TPU v7x, 128 devices: a whole 4x4x4 slice. The times are simulated.
128 devices in a mesh: gx: 16 (over z, x_hi, core), gy: 8 (over x_lo, y).
Axes of the slice: x: 4 (x_hi: 2, x_lo: 2; x = x_hi * 2 + x_lo), y: 4, z: 4, core: 2. Of those that a mesh axis runs over, the one named last changes fastest.
Arguments:
- grid_field: bfloat16 [1, 20, 2048, 2048], P(None, None, 'gx', 'gy'), may hold values from -8 to 8
- spectral_weight: float32 [2, 2, 20, 20, 2048], P(None, None, None, None, ('gx', 'gy')), may hold values from -1 to 1
- conv_near: bfloat16 [2, 20, 180], replicated, may hold values from -0.4375 to 0.4375
- conv_far: bfloat16 [2, 20, 500], replicated, may hold values from -0.25 to 0.25
- mix_logits: float32 [2, 3], replicated, may hold values from -1 to 1
- channel_bias: float32 [2, 20], replicated, may hold values from -3 to 3
Outputs:
- result_field: bfloat16 [1, 20, 2048, 2048], P(None, None, 'gx', 'gy')
All inputs are finite; a program needn't handle non-finite values.
Results may differ from a plain program's by a relative error of at most 0.004.
Values may be sent and summed in bfloat16 or wider, within the bound.
No kernel may reach another device: no remote copies, remote signals or barrier semaphores. Data moves between devices by JAX's collectives and lax.ppermute only.
A program may use at most 192 MiB of HBM per device.

v0:
```python
import math
import jax
import jax.numpy as jnp
from jax import lax
from jax.sharding import PartitionSpec as P

NX = 2048
NY = 2048
MX = 32
MY = 32
LAYERS = 2
KX = 64
MODES = 2048
full_turn = 2.0 * math.pi
highest = lax.Precision.HIGHEST


def padded_2(value, sides, width):
    for axis, dim in sides:
        size, length = (lax.axis_size(axis), value.shape[dim])
        up = [(i, (i + 1) % size) for i in range(size)]
        down = [(j, i) for i, j in up]
        last = lax.slice_in_dim(value, length - width, length, axis=dim)
        first = lax.slice_in_dim(value, 0, width, axis=dim)
        before = lax.ppermute(last, axis, up)
        after = lax.ppermute(first, axis, down)
        value = jnp.concatenate([before, value, after], axis=dim)
    return value


def forward_table(positions):
    col_modes = jnp.arange(MY, dtype=jnp.int32)
    phases = (positions[:, None] * col_modes[None, :] % NY).astype(jnp.float32) * (full_turn / NY)
    return jnp.concatenate([jnp.cos(phases), -jnp.sin(phases)], axis=1).astype(jnp.bfloat16)


def row_tables(positions):
    lower = jnp.arange(MX, dtype=jnp.int32)
    row_modes = jnp.concatenate([lower, lower + (NX - MX)])
    phases = (positions[:, None] * row_modes[None, :] % NX).astype(jnp.float32) * (full_turn / NX)
    return (jnp.cos(phases), jnp.sin(phases))


def inverse_table(positions):
    col_modes = jnp.arange(MY, dtype=jnp.int32)
    col_weight = jnp.where(col_modes == 0, 1.0, 2.0).astype(jnp.float32) / (NX * NY)
    phases = (col_modes[:, None] * positions[None, :] % NY).astype(jnp.float32) * (full_turn / NY)
    return jnp.concatenate(
        [jnp.cos(phases) * col_weight[:, None], -jnp.sin(phases) * col_weight[:, None]], axis=0
    )


def conv_rows(padded_plane, tap_weights, dilation, side_taps, first_row, count_rows, local_cols):
    channels = padded_plane.shape[0]
    pieces = []
    for row_tap in range(side_taps):
        for col_tap in range(side_taps):
            row_offset = 4 + (row_tap - side_taps // 2) * dilation + first_row
            col_offset = 4 + (col_tap - side_taps // 2) * dilation
            pieces.append(
                padded_plane[
                    :, row_offset : row_offset + count_rows, col_offset : col_offset + local_cols
                ]
            )
    stacked = jnp.stack(pieces, 0)
    shaped_weights = tap_weights.reshape(channels, side_taps * side_taps, channels)
    return jnp.einsum("otc,tcxy->oxy", shaped_weights, stacked, preferred_element_type=jnp.float32)


def on_device(grid_field, spectral_weight, conv_near, conv_far, mix_logits, channel_bias):
    channels = grid_field.shape[1]
    local_rows = grid_field.shape[2]
    local_cols = grid_field.shape[3]
    row_positions = lax.axis_index("gx") * local_rows + jnp.arange(local_rows, dtype=jnp.int32)
    col_positions = lax.axis_index("gy") * local_cols + jnp.arange(local_cols, dtype=jnp.int32)
    forward_cols = forward_table(col_positions)
    cosine_rows, sine_rows = row_tables(row_positions)
    inverse_cols = inverse_table(col_positions)
    share_modes = spectral_weight.shape[-1]
    owner_index = lax.axis_index("gx") * lax.axis_size("gy") + lax.axis_index("gy")
    mode_start = owner_index * share_modes
    row_blocks = max(1, local_rows // 32)
    while local_rows % row_blocks != 0:
        row_blocks = row_blocks - 1
    block_rows = local_rows // row_blocks
    planes_block = grid_field
    for layer_index in range(LAYERS):
        planes_here = planes_block.shape[0]
        line_sums = jnp.dot(
            planes_block.reshape(planes_here * channels * local_rows, local_cols),
            forward_cols,
            preferred_element_type=jnp.float32,
        )
        line_sums = line_sums.reshape(planes_here, channels, local_rows, 2 * MY)
        real_lines = line_sums[..., :MY]
        imaginary_lines = line_sums[..., MY:]

        def contract_rows(operand, lookup):
            return jnp.einsum("pcxk,xj->pcjk", operand, lookup, precision=highest)

        real_spec = contract_rows(real_lines, cosine_rows) + contract_rows(
            imaginary_lines, sine_rows
        )
        imaginary_spec = contract_rows(imaginary_lines, cosine_rows) - contract_rows(
            real_lines, sine_rows
        )
        partial_value = jnp.stack(
            [
                real_spec.reshape(planes_here, channels, MODES),
                imaginary_spec.reshape(planes_here, channels, MODES),
            ]
        )
        totals = lax.psum(partial_value, ("gx", "gy"))
        own_modes = lax.dynamic_slice_in_dim(totals, mode_start, share_modes, 3)

        def mix_modes(spectrum, weights):
            return jnp.einsum("pcm,com->pom", spectrum, weights, precision=highest)

        weight_real = spectral_weight[layer_index, 0]
        weight_imaginary = spectral_weight[layer_index, 1]
        real_mixed = mix_modes(own_modes[0], weight_real) - mix_modes(
            own_modes[1], weight_imaginary
        )
        imaginary_mixed = mix_modes(own_modes[1], weight_real) + mix_modes(
            own_modes[0], weight_imaginary
        )
        own_block = jnp.stack([real_mixed, imaginary_mixed])[None]
        gathered = lax.all_gather(own_block, ("gx", "gy"), axis=0, tiled=True)
        gathered = jnp.transpose(gathered, (1, 2, 3, 0, 4)).reshape(2, planes_here, channels, MODES)
        real_full = gathered[0].reshape(planes_here, channels, KX, MY)
        imaginary_full = gathered[1].reshape(planes_here, channels, KX, MY)

        def expand_rows(spectrum, lookup):
            return jnp.einsum("pcjk,xj->pcxk", spectrum, lookup, precision=highest)

        real_rows = expand_rows(real_full, cosine_rows) - expand_rows(imaginary_full, sine_rows)
        imaginary_rows = expand_rows(real_full, sine_rows) + expand_rows(
            imaginary_full, cosine_rows
        )
        stacked = jnp.concatenate([real_rows, imaginary_rows], axis=-1).reshape(
            planes_here * channels * local_rows, 2 * MY
        )
        spectral = jnp.dot(stacked, inverse_cols, precision=highest)
        layer_spectral = spectral.reshape(planes_here, channels, local_rows, local_cols)
        padded = padded_2(planes_block, (("gx", 2), ("gy", 3)), 4)
        exponents = jnp.exp(mix_logits[layer_index])
        mixture = exponents / jnp.sum(exponents)
        bias_column = channel_bias[layer_index][:, None, None]
        row_pieces = []
        for block_index in range(row_blocks):
            first_row = block_index * block_rows
            near_term = conv_rows(
                padded[0], conv_near[layer_index], 1, 3, first_row, block_rows, local_cols
            )
            far_term = conv_rows(
                padded[0], conv_far[layer_index], 2, 5, first_row, block_rows, local_cols
            )
            spectral_rows = layer_spectral[0, :, first_row : first_row + block_rows, :]
            summed = (
                mixture[0] * spectral_rows
                + mixture[1] * near_term
                + mixture[2] * far_term
                + bias_column
            )
            row_pieces.append(jax.nn.gelu(summed, approximate=False).astype(jnp.bfloat16))
        outputs = [jnp.concatenate(row_pieces, axis=1)]
        planes_block = jnp.stack(outputs)
    return planes_block


def solution(mesh):
    in_specs = (
        P(None, None, "gx", "gy"),
        P(None, None, None, None, ("gx", "gy")),
        P(),
        P(),
        P(),
        P(),
    )
    out_specs = P(None, None, "gx", "gy")
    return jax.shard_map(
        on_device, mesh=mesh, in_specs=in_specs, out_specs=out_specs, check_vma=False
    )
```

profile of v0, /device:TPU:0, one launch (start us, length us, event | category | flops | bytes accessed | tf_op | source)
XLA Modules:
  0.0 1025.7 jit_solution(15079216024907753427)
XLA Ops:
  8.8 6.0 collective-permute-start.1
  15.0 1.9 convolution_bitcast_fusion
  23.0 2.0 slice_bitcast_fusion.263
  27.7 2.0 broadcast_divide_fusion.1
  37.3 2.9 collective-permute-start.3
  40.8 1.7 reshape_squeeze.9
  71.0 3.8 copy-done.15
  74.8 14.7 %constant_dynamic-update-slice_fusion.20 = (bf16[25,20,32,256]{3,1,2,0:T(8,128)(2,1)}, bf16[25,20,32,256]{3,1,2,0:T(8,128)(2,1)S(1)}, bf16[9,20,32,256]{3,1,2,0:...) fusion(bf16[25,20,32,256]{3,1,2,0:T(8,128)(2,1)} %get-tuple-ele, ...), kind=kLoop, calls=%fused_computation.275 | loop fusion | bytes 5505024
  89.7 1.9 constant_dynamic-update-slice_fusion.19
  91.6 1.9 constant_dynamic-update-slice_fusion.18
  93.4 1.7 constant_dynamic-update-slice_fusion.17
  96.6 1.9 constant_dynamic-update-slice_fusion.15
  98.5 1.8 constant_dynamic-update-slice_fusion.14
  100.3 1.8 constant_dynamic-update-slice_fusion.13
  104.6 2.3 convolution_bitcast_fusion.3
  106.9 2.4 convolution_bitcast_fusion.5
  109.3 6.5 convolution_bitcast_fusion.7
  115.8 2.3 convolution_bitcast_fusion.9
  124.9 39.9 %all-reduce.3.cloned.1.call-done = f32[2,1,20,2048]{3,0,2,1:T(2,128)} async-done(((f32[2,1,20,2048]{3,0,2,1:T(2,128)}), f32[2,1,20,2048]{3,0,2,1:T(2,128)}) %all-reduce.3.cloned.1.call-update) | async-done | bytes 327696 | tf_op jit(solution)/shard_map/psum | solution.py:113
  167.1 326.2 %all-gather = f32[256,1,20,16]{2,3,1,0:T(8,128)S(1)} all-gather(f32[2,1,20,16]{2,3,1,0:T(8,128)S(1)} %pad_maximum_fusion.8), channel_id=2, replica_groups=mesh['gx'=16,'gy'=8] {'gx','gy'}, dimensions={0}, use_global_device_ids=true | all-gather | bytes 330240 | tf_op jit(solution)/shard_map/all_gather | solution.py:128
  500.9 2.2 convolution_bitcast_fusion.2
  503.2 10.4 %fusion.42 = (bf16[20,32,256]{2,1,0:T(8,128)(2,1)S(1)}, bf16[20,32,256]{2,1,0:T(8,128)(2,1)S(1)}, bf16[20,32,256]{2,1,0:T(8,128)(2,1)S(1)}, bf16[20,32,256]{2,1,0:T(8,128)(2,1)S(1)}) fusion(f32[32,256,20]{1,2,0:T(8,128)} %convolution_bitcast_fusion.9, f32[32,256,20]{1,2,0:T(8,128)} %convolution_bitcast_fusion.10, ...), kind=kLoop, calls=%fused_computation.51 | loop fusion | flops 46530560 | bytes 9175132 | tf_op jit(solution)/shard_map/convert_element_type | solution.py:165
  516.9 5.3 collective-permute-start.5
  526.1 4.3 collective-permute-start.7
  532.6 1.8 maximum_bitcast_fusion.1
  548.7 3.2 copy-done.18
  552.0 2.1 constant_dynamic-update-slice_fusion.147
  554.4 2.9 constant_dynamic-update-slice_fusion.146
  557.2 2.7 constant_dynamic-update-slice_fusion.145
  560.0 2.6 constant_dynamic-update-slice_fusion.144
  562.6 2.9 constant_dynamic-update-slice_fusion.143
  565.5 2.6 constant_dynamic-update-slice_fusion.142
  568.1 2.6 constant_dynamic-update-slice_fusion.141
  570.7 2.6 constant_dynamic-update-slice_fusion.140
  573.2 2.5 constant_dynamic-update-slice_fusion.139
  576.2 2.8 copy-done.16
  579.2 4.5 fusion.25
  583.7 9.6 fusion.19
  593.3 5.3 fusion.22
  598.6 5.3 fusion.16
  603.8 2.6 fusion.28
  606.4 2.8 fusion.31
  609.2 2.6 fusion.34
  611.7 2.6 fusion.37
  614.3 58.0 %all-reduce.5.cloned.1.call-done = f32[2,1,20,2048]{3,0,2,1:T(2,128)} async-done(((f32[2,1,20,2048]{3,0,2,1:T(2,128)}), f32[2,1,20,2048]{3,0,2,1:T(2,128)}) %all-reduce.5.cloned.1.call-update) | async-done | bytes 327696 | tf_op jit(solution)/shard_map/psum | solution.py:113
  674.7 325.8 %all-gather.1 = f32[256,1,20,16]{2,3,1,0:T(8,128)S(1)} all-gather(f32[2,1,20,16]{2,3,1,0:T(8,128)S(1)} %pad_maximum_fusion.9), channel_id=3, replica_groups=mesh['gx'=16,'gy'=8] {'gx','gy'}, dimensions={0}, use_global_device_ids=true | all-gather | bytes 330240 | tf_op jit(solution)/shard_map/all_gather | solution.py:128
  1004.6 2.2 convolution_bitcast_fusion.1
  1006.8 10.5 %fusion.54 = (bf16[20,32,256]{2,1,0:T(8,128)(2,1)S(1)}, bf16[20,32,256]{2,1,0:T(8,128)(2,1)S(1)}, bf16[20,32,256]{2,1,0:T(8,128)(2,1)S(1)}, bf16[20,32,256]{2,1,0:T(8,128)(2,1)S(1)}) fusion(f32[32,256,20]{1,2,0:T(8,128)} %fusion.16, f32[32,256,20]{1,2,0:T(8,128)} %fusion.28, f32[1,20,128,256]{3,2,1,0:T(8,128)S(1)} %convolution_bitcast_fusion.1, ...), kind=kLoop, calls=%fused_computation.63 | loop fusion | flops 46530560 | bytes 9175132 | tf_op jit(solution)/shard_map/convert_element_type | solution.py:165
  (225 shorter events, 100.2 us)
Async XLA Ops:
  6.5 15.6 %copy-start.8 = (bf16[2,20,500]{2,0,1:T(2,128)(2,1)S(1)}, bf16[2,20,500]{2,0,1:T(2,128)(2,1)}, u32[]{:S(2)}) copy-start(bf16[2,20,500]{2,0,1:T(2,128)(2,1)} %param.9) | copy-start | bytes 120004
  6.5 158.2 %all-reduce.3.cloned.1.call-start = ((), (), s32[]{:S(2)}) async-start(), calls=%async_computation | async-start | bytes 655360 | tf_op jit(solution)/shard_map/psum | solution.py:113
  8.1 23.0 %collective-permute-start = (bf16[1,20,4,256]{3,1,2,0:T(8,128)(2,1)}, bf16[1,20,4,256]{3,1,2,0:T(8,128)(2,1)}, u32[]{:S(2)}, u32[]{:S(2)}) collective-permute-start(bf16[1,20,4,256]{3,1,2,0:T(8,128)(2,1)} %copy.500), channel_id=1, source_target_pairs={{0,8},{8,16},{16,24},{24,32},{32,40},{40,48},{48,56},{56,64},{64,7... | collective-permute-start | bytes 122888 | tf_op jit(solution)/shard_map/ppermute | solution.py:25
  8.8 24.0 %collective-permute-start.1 = (bf16[1,20,4,256]{3,1,2,0:T(8,128)(2,1)}, bf16[1,20,4,256]{3,1,2,0:T(8,128)(2,1)}, u32[]{:S(2)}, u32[]{:S(2)}) collective-permute-start(bf16[1,20,4,256]{3,1,2,0:T(8,128)(2,1)} %copy.501), channel_id=1, source_target_pairs={{8,0},{16,8},{24,16},{32,24},{40,32},{48,40},{56,48},{64,56},{72,6... | collective-permute-start | bytes 122888 | tf_op jit(solution)/shard_map/ppermute | solution.py:26
  15.0 7.2 copy-start.11
  15.0 7.2 copy-start.13
  15.0 10.7 %copy-start.19 = (f32[2,3]{1,0:T(2,128)S(1)}, f32[2,3]{1,0:T(2,128)}, u32[]{:S(2)}) copy-start(f32[2,3]{1,0:T(2,128)} %param.10) | copy-start | bytes 76
  15.0 17.0 %copy-start = (bf16[1,20,128,256]{3,2,1,0:T(8,128)(2,1)S(1)}, bf16[1,20,128,256]{3,2,1,0:T(8,128)(2,1)}, u32[]{:S(2)}) copy-start(bf16[1,20,128,256]{3,2,1,0:T(8,128)(2,1)} %param.6) | copy-start | bytes 3932164
  22.1 650.2 %all-reduce.5.cloned.1.call-start = ((), (), s32[]{:S(2)}) async-start(), calls=%async_computation.1 | async-start | bytes 655360 | tf_op jit(solution)/shard_map/psum | solution.py:113
  35.1 12.2 %collective-permute-start.2 = (bf16[1,20,136,4]{2,3,1,0:T(4,128)(2,1)}, bf16[1,20,136,4]{2,3,1,0:T(4,128)(2,1)S(1)}, u32[]{:S(2)}, u32[]{:S(2)}) collective-permute-start(bf16[1,20,136,4]{2,3,1,0:T(4,128)(2,1)} %copy.211), channel_id=1, source_target_pairs={{0,1},{1,2},{2,3},{3,4},{4,5},{5,6},{6,7},{7,0},{8,9},{9,10},{10,1... | collective-permute-start | bytes 65288 | tf_op jit(solution)/shard_map/ppermute | solution.py:25
  37.3 10.6 %collective-permute-start.3 = (bf16[1,20,136,4]{2,3,1,0:T(4,128)(2,1)S(1)}, bf16[1,20,136,4]{2,3,1,0:T(4,128)(2,1)}, u32[]{:S(2)}, u32[]{:S(2)}) collective-permute-start(bf16[1,20,136,4]{2,3,1,0:T(4,128)(2,1)S(1)} %copy.212), channel_id=1, source_target_pairs={{1,0},{2,1},{3,2},{4,3},{5,4},{6,5},{7,6},{0,7},{9,8},{10,9},{11,1... | collective-permute-start | bytes 65288 | tf_op jit(solution)/shard_map/ppermute | solution.py:26
  71.0 3.8 copy-start.15
  100.3 4.3 copy-start.7
  106.9 8.9 slice-start
  106.9 8.9 slice-start.1
  109.3 6.5 slice-start.2
  115.8 2.4 copy-start.5
  120.4 45.4 %copy-start.4 = (f32[20,20,16]{1,2,0:T(8,128)S(1)}, f32[20,20,16]{1,2,0:T(8,128)}, u32[]{:S(2)}) copy-start(f32[20,20,16]{1,2,0:T(8,128)} %get-tuple-element.287) | copy-start | bytes 76804
  120.4 46.1 %copy-start.3 = (f32[20,20,16]{1,2,0:T(8,128)S(1)}, f32[20,20,16]{1,2,0:T(8,128)}, u32[]{:S(2)}) copy-start(f32[20,20,16]{1,2,0:T(8,128)} %get-tuple-element.286) | copy-start | bytes 76804
  124.9 376.1 %copy-start.6 = (f32[32,256]{1,0:T(8,128)S(1)}, f32[32,256]{1,0:T(8,128)}, u32[]{:S(2)}) copy-start(f32[32,256]{1,0:T(8,128)} %get-tuple-element.296) | copy-start | bytes 98308
  167.1 336.1 %copy-start.21 = (f32[20]{0:T(128)S(1)}, f32[20]{0:T(128)}, u32[]{:S(2)}) copy-start(f32[20]{0:T(128)} %get-tuple-element.300) | copy-start | bytes 244
  494.2 9.0 copy-start.1
  500.9 12.8 %copy-start.12 = (bf16[256,32]{0,1:T(8,128)(2,1)S(1)}, bf16[256,32]{0,1:T(8,128)(2,1)}, u32[]{:S(2)}) copy-start(bf16[256,32]{0,1:T(8,128)(2,1)} %copy-done.11) | copy-start | bytes 49156
  500.9 12.8 %copy-start.14 = (bf16[256,32]{0,1:T(8,128)(2,1)S(1)}, bf16[256,32]{0,1:T(8,128)(2,1)}, u32[]{:S(2)}) copy-start(bf16[256,32]{0,1:T(8,128)(2,1)} %copy-done.13) | copy-start | bytes 49156
  516.8 7.1 collective-permute-start.4
  516.9 7.0 collective-permute-start.5
  525.6 6.2 collective-permute-start.6
  526.1 6.0 collective-permute-start.7
  548.7 3.2 copy-start.18
  568.1 11.1 %copy-start.9 = (bf16[20,25,20]{1,0,2:T(8,128)(2,1)S(1)}, bf16[20,25,20]{1,0,2:T(8,128)(2,1)}, u32[]{:S(2)}) copy-start(bf16[20,25,20]{1,0,2:T(8,128)(2,1)} %copy.257) | copy-start | bytes 60004
  575.7 3.3 copy-start.16
  583.7 9.6 copy-start.17
  598.6 5.3 copy-start.10
  606.4 66.9 %copy-start.2 = (f32[20,20,16]{1,2,0:T(8,128)S(1)}, f32[20,20,16]{1,2,0:T(8,128)}, u32[]{:S(2)}) copy-start(f32[20,20,16]{1,2,0:T(8,128)} %get-tuple-element.285) | copy-start | bytes 76804
  674.7 332.2 %copy-start.20 = (f32[20]{0:T(128)S(1)}, f32[20]{0:T(128)}, u32[]{:S(2)}) copy-start(f32[20]{0:T(128)} %get-tuple-element.299) | copy-start | bytes 244
Sparse Core Ops, SparseCore 0:
  22.2 142.4 all-reduce.2
  531.7 140.5 all-reduce.4
where the time goes:
time: 1030 us
  blocking collectives  652 us (63%)
  local copies, waits for them, and re-layouts  131 us (13%)
  waiting for transfers between devices  98.6 us (10%)
  matrix products  74.6 us (7%)
  other arithmetic  34.5 us (3%)
  starting transfers between devices  20.3 us (2%)
  between operations  14.7 us (1%)
    all_gather x2, blocking collectives, on_device(): gathered = lax.all_gather(own_block, ('gx', 'gy'), axis=0, tiled=True)  652 us
    unnamed x121, local copies, waits for them, and re-layouts  98.1 us
    psum x2, waiting for transfers between devices, on_device(): totals = lax.psum(partial_value, ('gx', 'gy'))  97.8 us
    dot_general x16, matrix products, conv_rows(): jnp.einsum('otc,tcxy->oxy', shaped_weights, stacked, preferred_element_ty...  53.9 us
    convert_element_type x2, other arithmetic, on_device(): jax.nn.gelu(summed, approximate=False).astype(jnp.bfloat16)  20.9 us
  transfers between devices with their start and end apart: 10, of which 4 were waited for; matrix products, arithmetic and copies ran while one was open for 18% of the time, Pallas kernels for 0%

commit v1 on v0

--- a/solution.py
+++ b/solution.py
@@ -110,7 +110,7 @@
                 imaginary_spec.reshape(planes_here, channels, MODES),
             ]
         )
-        totals = lax.psum(partial_value, ("gx", "gy"))
+        totals = jnp.sum(lax.all_gather(partial_value, ("gx", "gy")), axis=0)
         own_modes = lax.dynamic_slice_in_dim(totals, mode_start, share_modes, 3)
 
         def mix_modes(spectrum, weights):

time: 1030 us -> 1560 us (1.51)
  waiting for transfers between devices: 98.6 us -> 535 us
  local copies, waits for them, and re-layouts: 131 us -> 185 us
  other arithmetic: 34.5 us -> 68.5 us
    all_gather x0 -> x2, waiting for transfers between devices: none -> 529 us  [on_device(): totals = jnp.sum(lax.all_gather(partial_value, ('gx', 'gy')), axis=0)]
    psum x2 -> x0, waiting for transfers between devices: 97.8 us -> none  [on_device(): totals = lax.psum(partial_value, ('gx', 'gy'))]
    unnamed x121 -> x129, local copies, waits for them, and re-layouts: 98.1 us -> 157 us
    reduce_sum x0 -> x2, other arithmetic: none -> 35.6 us  [on_device(): totals = jnp.sum(lax.all_gather(partial_value, ('gx', 'gy')), axis=0)]
  transfers between devices with their start and end apart: 10 -> 10, of which waited for: 4 -> 6; matrix products, arithmetic and copies ran while one was open for 18% -> 10% of each run, Pallas kernels for 0% -> 0%
where the time goes in v1:
time: 1560 us; the launch traced here: 1550 us
  blocking collectives  657 us (42%)
  waiting for transfers between devices  535 us (34%)
  local copies, waits for them, and re-layouts  185 us (12%)
  matrix products  70.6 us (5%)
  other arithmetic  68.5 us (4%)
  starting transfers between devices  19.6 us (1%)
    all_gather x2, blocking collectives, on_device(): gathered = lax.all_gather(own_block, ('gx', 'gy'), axis=0, tiled=True)  657 us
    all_gather x2, waiting for transfers between devices, on_device(): totals = jnp.sum(lax.all_gather(partial_value, ('gx', 'gy')), axis=0)  529 us
    unnamed x129, local copies, waits for them, and re-layouts  157 us
    dot_general x16, matrix products, conv_rows(): jnp.einsum('otc,tcxy->oxy', shaped_weights, stacked, preferred_element_ty...  49.9 us
    reduce_sum x2, other arithmetic, on_device(): totals = jnp.sum(lax.all_gather(partial_value, ('gx', 'gy')), axis=0)  35.6 us
  transfers between devices with their start and end apart: 10, of which 6 were waited for; matrix products, arithmetic and copies ran while one was open for 10% of the time, Pallas kernels for 0%

profile of v1, /device:TPU:0, one launch (start us, length us, event | category | flops | bytes accessed | tf_op | source)
XLA Modules:
  0.0 1550.5 jit_solution(7015743341356248317)
XLA Ops:
  6.8 2.0 convolution_bitcast_fusion
  14.5 6.1 collective-permute-start.1
  24.6 2.0 slice_bitcast_fusion.263
  31.0 3.4 collective-permute-start.3
  37.7 3.4 collective-permute-done.2
  63.9 2.0 constant_dynamic-update-slice_fusion.22
  66.7 3.8 copy-done.18
  70.5 1.8 constant_dynamic-update-slice_fusion.20
  72.5 1.9 constant_dynamic-update-slice_fusion.19
  74.4 1.8 constant_dynamic-update-slice_fusion.18
  79.4 1.9 constant_dynamic-update-slice_fusion.15
  83.1 1.8 constant_dynamic-update-slice_fusion.13
  92.6 6.5 convolution_bitcast_fusion.9
  99.1 2.4 convolution_bitcast_fusion.5
  101.5 2.4 convolution_bitcast_fusion.7
  103.9 2.4 convolution_bitcast_fusion.3
  106.3 269.2 %all-gather.7.cloned.1.call-done = f32[256,1,20,2048]{3,1,2,0:T(1,128)} async-done(((f32[2,1,20,2048]{3,1,2,0:T(1,128)}), f32[256,1,20,2048]{3,1,2,0:T(1,128)}) %all-gather.7.cloned.1.call-update) | async-done | bytes 41943056 | tf_op jit(solution)/shard_map/all_gather | solution.py:113
  375.5 38.0 %copy.418 = f32[256,1,20,2048]{3,2,1,0:T(8,128)} copy(f32[256,1,20,2048]{3,1,2,0:T(1,128)} %all-gather.7.cloned.1.call-done) | data formatting | bytes 83886080
  413.4 17.8 %bitcast_reduce_fusion.1 = f32[2,20,2048]{2,1,0:T(8,128)S(1)} fusion(f32[128,2,20,2048]{3,2,1,0:T(8,128)} %bitcast.1571), kind=kLoop, calls=%fused_computation.1 | loop fusion | flops 10403840 | bytes 42270720 | tf_op jit(solution)/shard_map/reduce_sum | solution.py:113
  432.8 328.6 %all-gather.1 = f32[256,1,20,16]{2,3,1,0:T(8,128)S(1)} all-gather(f32[2,1,20,16]{2,3,1,0:T(8,128)S(1)} %pad_maximum_fusion.8), channel_id=3, replica_groups=mesh['gx'=16,'gy'=8] {'gx','gy'}, dimensions={0}, use_global_device_ids=true | all-gather | bytes 330240 | tf_op jit(solution)/shard_map/all_gather | solution.py:128
  767.3 3.0 convolution_bitcast_fusion.2
  770.3 10.9 fusion.42
  788.2 5.3 collective-permute-start.5
  797.7 4.3 collective-permute-start.7
  804.4 1.8 maximum_bitcast_fusion.1
  820.7 3.3 copy-done.19
  823.9 2.1 constant_dynamic-update-slice_fusion.147
  826.3 2.9 constant_dynamic-update-slice_fusion.146
  829.2 2.7 constant_dynamic-update-slice_fusion.145
  831.9 2.6 constant_dynamic-update-slice_fusion.144
  834.5 2.9 constant_dynamic-update-slice_fusion.143
  837.4 2.6 constant_dynamic-update-slice_fusion.142
  840.0 2.6 constant_dynamic-update-slice_fusion.141
  842.6 2.6 constant_dynamic-update-slice_fusion.140
  845.2 2.5 constant_dynamic-update-slice_fusion.139
  850.0 2.7 fusion.37
  852.7 2.6 fusion.34
  855.3 2.6 fusion.31
  857.9 5.3 fusion.22
  863.2 5.5 fusion.19
  868.7 5.3 fusion.16
  873.9 5.3 fusion.25
  879.3 259.7 %all-gather.9.cloned.1.call-done = f32[256,1,20,2048]{3,1,2,0:T(1,128)} async-done(((f32[2,1,20,2048]{3,1,2,0:T(1,128)}), f32[256,1,20,2048]{3,1,2,0:T(1,128)}) %all-gather.9.cloned.1.call-update) | async-done | bytes 41943056 | tf_op jit(solution)/shard_map/all_gather | solution.py:113
  1139.0 38.2 %copy.419 = f32[256,1,20,2048]{3,2,1,0:T(8,128)} copy(f32[256,1,20,2048]{3,1,2,0:T(1,128)} %all-gather.9.cloned.1.call-done) | data formatting | bytes 83886080
  1177.2 17.8 %bitcast_reduce_fusion = f32[2,20,2048]{2,1,0:T(8,128)S(1)} fusion(f32[128,2,20,2048]{3,2,1,0:T(8,128)} %bitcast.1572), kind=kLoop, calls=%fused_computation | loop fusion | flops 10403840 | bytes 42270720 | tf_op jit(solution)/shard_map/reduce_sum | solution.py:113
  1196.6 328.4 %all-gather.3 = f32[256,1,20,16]{2,3,1,0:T(8,128)S(1)} all-gather(f32[2,1,20,16]{2,3,1,0:T(8,128)S(1)} %pad_maximum_fusion.9), channel_id=5, replica_groups=mesh['gx'=16,'gy'=8] {'gx','gy'}, dimensions={0}, use_global_device_ids=true | all-gather | bytes 330240 | tf_op jit(solution)/shard_map/all_gather | solution.py:128
  1529.2 2.2 convolution_bitcast_fusion.1
  1531.5 10.5 fusion.54
  (238 shorter events, 98.1 us)
Async XLA Ops:
  6.5 7.7 copy-start
  6.5 368.9 %all-gather.7.cloned.1.call-start = ((), (), s32[]{:S(2)}) async-start(), calls=%async_computation | async-start | bytes 42270720 | tf_op jit(solution)/shard_map/all_gather | solution.py:113
  6.7 7.6 copy-start.13
  6.7 7.6 copy-start.15
  6.7 13.8 copy-start.20
  6.7 14.4 copy-start.11
  6.8 15.2 copy-start.22
  14.2 1124.8 %all-gather.9.cloned.1.call-start = ((), (), s32[]{:S(2)}) async-start(), calls=%async_computation.1 | async-start | bytes 42270720 | tf_op jit(solution)/shard_map/all_gather | solution.py:113
  14.4 13.7 collective-permute-start
  14.5 14.4 collective-permute-start.1
  31.0 10.7 collective-permute-start.3
  34.4 6.8 collective-permute-start.2
  66.7 3.8 copy-start.18
  83.1 4.3 copy-start.7
  87.3 5.2 copy-start.10
  92.6 8.9 slice-start
  92.6 8.9 slice-start.1
  99.1 2.4 slice-start.2
  413.4 18.3 %copy-start.4 = (f32[20,20,16]{1,2,0:T(8,128)S(1)}, f32[20,20,16]{1,2,0:T(8,128)}, u32[]{:S(2)}) copy-start(f32[20,20,16]{1,2,0:T(8,128)} %get-tuple-element.287) | copy-start | bytes 76804
  762.2 8.0 copy-start.1
  765.5 15.7 %copy-start.14 = (bf16[256,32]{0,1:T(8,128)(2,1)S(1)}, bf16[256,32]{0,1:T(8,128)(2,1)}, u32[]{:S(2)}) copy-start(bf16[256,32]{0,1:T(8,128)(2,1)} %copy-done.13) | copy-start | bytes 49156
  765.5 15.7 %copy-start.16 = (bf16[256,32]{0,1:T(8,128)(2,1)S(1)}, bf16[256,32]{0,1:T(8,128)(2,1)}, u32[]{:S(2)}) copy-start(bf16[256,32]{0,1:T(8,128)(2,1)} %copy-done.15) | copy-start | bytes 49156
  781.2 3.1 copy-start.5
  781.2 3.1 copy-start.6
  784.3 17.7 %copy-start.17 = (bf16[20,180]{1,0:T(8,128)(2,1)S(1)}, bf16[20,180]{1,0:T(8,128)(2,1)}, u32[]{:S(2)}) copy-start(bf16[20,180]{1,0:T(8,128)(2,1)} %get-tuple-element.7) | copy-start | bytes 21604
  784.3 17.8 %copy-start.12 = (bf16[20,500]{1,0:T(8,128)(2,1)S(1)}, bf16[20,500]{1,0:T(8,128)(2,1)}, u32[]{:S(2)}) copy-start(bf16[20,500]{1,0:T(8,128)(2,1)} %get-tuple-element.5) | copy-start | bytes 60004
  788.1 7.1 collective-permute-start.4
  788.2 7.2 collective-permute-start.5
  797.1 6.4 collective-permute-start.6
  797.7 6.3 collective-permute-start.7
  820.6 3.3 copy-start.19
  855.3 7.9 slice-start.3
  857.9 5.3 slice-start.4
  1177.2 18.0 %copy-start.2 = (f32[20,20,16]{1,2,0:T(8,128)S(1)}, f32[20,20,16]{1,2,0:T(8,128)}, u32[]{:S(2)}) copy-start(f32[20,20,16]{1,2,0:T(8,128)} %get-tuple-element.285) | copy-start | bytes 76804
  1177.2 18.3 %copy-start.3 = (f32[20,20,16]{1,2,0:T(8,128)S(1)}, f32[20,20,16]{1,2,0:T(8,128)}, u32[]{:S(2)}) copy-start(f32[20,20,16]{1,2,0:T(8,128)} %get-tuple-element.288) | copy-start | bytes 76804
  1195.0 334.2 %copy-start.8 = (f32[32,256]{1,0:T(8,128)S(1)}, f32[32,256]{1,0:T(8,128)}, u32[]{:S(2)}) copy-start(f32[32,256]{1,0:T(8,128)} %get-tuple-element.295) | copy-start | bytes 98308
  1195.0 334.2 %copy-start.9 = (f32[32,256]{1,0:T(8,128)S(1)}, f32[32,256]{1,0:T(8,128)}, u32[]{:S(2)}) copy-start(f32[32,256]{1,0:T(8,128)} %get-tuple-element.296) | copy-start | bytes 98308
  1196.6 334.9 %copy-start.21 = (f32[20]{0:T(128)S(1)}, f32[20]{0:T(128)}, u32[]{:S(2)}) copy-start(f32[20]{0:T(128)} %get-tuple-element.299) | copy-start | bytes 244
Sparse Core Ops, SparseCore 0:
  14.3 361.0 all-gather.6
  787.0 351.9 all-gather.8
